TPU v7x, 32 devices: a whole 2x2x4 slice. The times are simulated.
32 devices in a mesh: pipe: 4 (over x, core), tensor: 8 (over z, y).
Axes of the slice: x: 2, y: 2, z: 4, core: 2. Of those that a mesh axis runs over, the one named last changes fastest.
Arguments:
- hidden: bfloat16 [384, 8192], P('pipe', 'tensor'), may hold values from -64 to 64
- weight: bfloat16 [8192, 16384], P(None, ('pipe', 'tensor')), may hold values from -0.23201941 to 0.23201941
- targets: int32 [384], replicated, may hold values from 0 to 16383
- token_weight: float32 [384], replicated, may hold values from 0.1 to 1
Outputs:
- token_loss: float32 [384], P('pipe')
- hidden_grad: float32 [384, 8192], P('pipe', 'tensor')
All inputs are finite; a program needn't handle non-finite values.
Results may differ from a plain program's by a relative error of at most 0.0029.
Values may be sent and summed in bfloat16 or wider, within the bound.
A program may use at most 128 MiB of HBM per device.

v0:
```python
import jax
import jax.numpy as jnp
from jax import lax
from jax.sharding import PartitionSpec as P

loss_scale = 32.0


def local(hidden, weight, targets, token_weight):
    rows_local = hidden.shape[0]
    width_local = weight.shape[1]
    full_rows = lax.all_gather(hidden, "tensor", axis=1, tiled=True)
    logits = jnp.dot(
        lax.all_gather(full_rows, "pipe", axis=0, tiled=True),
        weight,
        preferred_element_type=jnp.float32,
    )
    device_block = lax.axis_index("pipe") * lax.axis_size("tensor") + lax.axis_index("tensor")
    columns = device_block * width_local + jnp.arange(width_local, dtype=jnp.int32)
    target_hit = targets[:, None] == columns[None, :]
    chosen = jnp.sum(jnp.where(target_hit, logits, jnp.float32(0.0)), axis=1)
    local_peak = jnp.max(logits, axis=1)
    global_peak = lax.pmax(local_peak, ("pipe", "tensor"))
    local_total = jnp.sum(jnp.exp(logits - global_peak[:, None]), axis=1)
    global_total, target_logit = lax.psum((local_total, chosen), ("pipe", "tensor"))
    log_total = global_peak + jnp.log(global_total)
    loss_rows = log_total - target_logit
    token_loss = lax.dynamic_slice_in_dim(
        loss_rows, lax.axis_index("pipe") * rows_local, rows_local, 0
    )
    softmax = jnp.exp(logits - log_total[:, None])
    dlogits = (
        loss_scale * token_weight[:, None] * (softmax - target_hit.astype(jnp.float32))
    ).astype(jnp.bfloat16)
    section_part = lax.psum_scatter(
        lax.dot_general(
            dlogits, weight, (((1,), (1,)), ((), ())), preferred_element_type=jnp.float32
        ),
        "pipe",
        scatter_dimension=0,
        tiled=True,
    )
    hidden_grad = lax.psum_scatter(section_part, "tensor", scatter_dimension=1, tiled=True)
    return (token_loss, hidden_grad)


def solution(mesh):
    in_specs = (P("pipe", "tensor"), P(None, ("pipe", "tensor")), P(), P())
    out_specs = (P("pipe"), P("pipe", "tensor"))
    return jax.shard_map(local, mesh=mesh, in_specs=in_specs, out_specs=out_specs, check_vma=False)
```

profile of v0, /device:TPU:0, one launch (start us, length us, event | category | flops | bytes accessed | tf_op | source)
XLA Modules:
  0.0 389.2 jit_solution(3919256009394892303)
XLA Ops:
  7.2 0.0 all-gather.3.cloned.1.call-start
  7.2 0.7 all-gather.3.cloned.1.call-update
  7.9 0.0 all-gather.5.cloned.1.call-start
  7.9 49.2 %all-gather.3.cloned.1.call-done = bf16[96,8192]{1,0:T(8,128)(2,1)} async-done(((bf16[96,1024]{1,0:T(8,128)(2,1)}), bf16[96,8192]{1,0:T(8,128)(2,1)}) %all-gather.3.cloned.1.call-update) | async-done | bytes 1572880 | tf_op jit(solution)/shard_map/all_gather | solution.py:12
  57.1 0.0 all-gather.5.cloned.1.call-update
  57.1 0.0 reduce-scatter.3.cloned.1.call-start
  57.2 0.7 broadcast_multiply_fusion
  57.9 0.0 copy-start
  57.9 45.5 %all-gather.5.cloned.1.call-done = bf16[384,8192]{1,0:T(8,128)(2,1)} async-done(((bf16[96,8192]{1,0:T(8,128)(2,1)}), bf16[384,8192]{1,0:T(8,128)(2,1)}) %all-gather.5.cloned.1.call-update) | async-done | bytes 6291472 | tf_op jit(solution)/shard_map/all_gather | solution.py:14
  103.4 8.0 %fusion.11 = (f32[384]{0:T(512)S(1)}, f32[384,512]{1,0:T(8,128)S(1)}) fusion(bf16[384,8192]{1,0:T(8,128)(2,1)} %all-gather.5.cloned.1.call-done, bf16[8192,512]{1,0:T(8,128)(2,1)} %param.5), kind=kOutput, calls=%fused_computation.16 | convolution fusion | flops 3221421568 | bytes 15468032 | tf_op jit(solution)/shard_map/dot_general | solution.py:13
  111.4 39.3 %pmax.7 = f32[384]{0:T(512)S(1)} all-reduce(f32[384]{0:T(512)S(1)} %get-tuple-element.8), channel_id=1, replica_groups=mesh['pipe'=4,'tensor'=8] {'pipe','tensor'}, use_global_device_ids=true, to_apply=%region_1.2 | all-reduce | flops 384 | bytes 3072 | tf_op jit(solution)/shard_map/pmax | solution.py:23
  150.7 0.0 copy-done
  150.7 0.3 fusion
  151.1 41.0 %all-reduce = (f32[384]{0:T(512)S(1)}, f32[384]{0:T(512)S(1)}) all-reduce(f32[384]{0:T(512)S(1)} %get-tuple-element.3, f32[384]{0:T(512)S(1)} %get-tuple-element.2), channel_id=1, replica_groups=mesh['pipe'=4,'tensor'=8] {'pipe','tensor'}, use_global_device_ids=true, to_apply=%region_3.4 | all-reduce | flops 768 | bytes 6144 | tf_op jit(solution)/shard_map/psum | solution.py:25
  192.1 12.0 %fusion.4 = f32[384,8192]{1,0:T(8,128)} fusion(bf16[8192,512]{1,0:T(8,128)(2,1)} %param.5, f32[384,512]{1,0:T(8,128)S(1)} %get-tuple-element.9, f32[384]{0:T(512)S(1)} %get-tuple-element.7, f32[384]{0:T(512)S(1)} %broadcast_multiply_fusion, s32[512]{0:T(512)S(1)} %iota_add_fusion, s32[384]{0:T(512)S(1)} %copy-done), kind=kOutput, calls=%fused_computation.7 | convolution fusion | flops 3222405120 | bytes 21764608 | tf_op jit(solution)/shard_map/dot_general | solution.py:36
  204.1 0.0 reduce-scatter.3.cloned.1.call-update
  204.1 0.0 reduce-scatter.5.cloned.1.call-start
  204.1 99.5 %reduce-scatter.3.cloned.1.call-done = f32[96,8192]{1,0:T(8,128)} async-done(((f32[384,8192]{1,0:T(8,128)}), f32[96,8192]{1,0:T(8,128)}) %reduce-scatter.3.cloned.1.call-update) | async-done | bytes 3145744 | tf_op jit(solution)/shard_map/reduce_scatter | solution.py:35
  303.6 0.0 reduce-scatter.5.cloned.1.call-update
  303.6 0.6 dynamic_slice.3
  304.2 78.4 %reduce-scatter.5.cloned.1.call-done = f32[96,1024]{1,0:T(8,128)} async-done(((f32[96,8192]{1,0:T(8,128)}), f32[96,1024]{1,0:T(8,128)}) %reduce-scatter.5.cloned.1.call-update) | async-done | bytes 393232 | tf_op jit(solution)/shard_map/reduce_scatter | solution.py:43
  (2 shorter events, 0.0 us)
Async XLA Ops:
  7.2 49.9 %all-gather.3.cloned.1.call-start = ((), (), s32[]{:S(2)}) async-start(), calls=%async_computation.2 | async-start | bytes 1769472 | tf_op jit(solution)/shard_map/all_gather | solution.py:12
  7.9 95.5 %all-gather.5.cloned.1.call-start = ((), (), s32[]{:S(2)}) async-start(), calls=%async_computation.3 | async-start | bytes 7864320 | tf_op jit(solution)/shard_map/all_gather | solution.py:14
  57.1 246.5 %reduce-scatter.3.cloned.1.call-start = ((), (), s32[]{:S(2)}) async-start(), calls=%async_computation.4 | async-start | bytes 15728640 | tf_op jit(solution)/shard_map/reduce_scatter | solution.py:35
  57.9 92.9 %copy-start = (s32[384]{0:T(512)S(1)}, s32[384]{0:T(512)}, u32[]{:S(2)}) copy-start(s32[384]{0:T(512)} %param.6) | copy-start | bytes 4612
  204.1 178.6 %reduce-scatter.5.cloned.1.call-start = ((), (), s32[]{:S(2)}) async-start(), calls=%async_computation.5 | async-start | bytes 3538944 | tf_op jit(solution)/shard_map/reduce_scatter | solution.py:43
Sparse Core Ops, SparseCore 0:
  10.2 46.9 all-gather.2
  58.7 44.7 all-gather.4
  204.2 99.3 reduce-scatter.2
  307.7 74.9 reduce-scatter.4
where the time goes:
time: 390 us; the launch traced here: 389 us
  waiting for transfers between devices  273 us (70%)
  blocking collectives  80.3 us (21%)
  matrix products  20 us (5%)
  between operations  13.8 us (4%)
    reduce_scatter x1, waiting for transfers between devices, local(): lax.psum_scatter(lax.dot_general(dlogits, weight, (((1,), (1,)), ((), ())...  99.5 us
    reduce_scatter x1, waiting for transfers between devices, local(): lax.psum_scatter(section_part, 'tensor', scatter_dimension=1, tiled=True)  78.4 us
    all_gather x1, waiting for transfers between devices, local(): full_rows = lax.all_gather(hidden, 'tensor', axis=1, tiled=True)  49.2 us
    all_gather x1, waiting for transfers between devices, local(): lax.all_gather(full_rows, 'pipe', axis=0, tiled=True)  45.5 us
    psum x1, blocking collectives, local(): lax.psum((local_total, chosen), ('pipe', 'tensor'))  41 us
    pmax x1, blocking collectives, local(): global_peak = lax.pmax(local_peak, ('pipe', 'tensor'))  39.3 us
    dot_general x1, matrix products, local(): lax.dot_general(dlogits, weight, (((1,), (1,)), ((), ())), preferred_elem...  12 us
    dot_general x1, matrix products, local(): jnp.dot(lax.all_gather(full_rows, 'pipe', axis=0, tiled=True), weight, pr...  8 us
  transfers between devices with their start and end apart: 4, of which 4 were waited for; matrix products, arithmetic and copies ran while one was open for 0% of the time, Pallas kernels for 0%

commit v1 on v0

v1 whole, which is shorter than its diff:
```python
import functools

import jax
import jax.numpy as jnp
from jax import lax
from jax.experimental import pallas as pl
from jax.experimental.pallas import tpu as pltpu
from jax.sharding import PartitionSpec as P

loss_scale = 32.0
f32, bf16 = jnp.float32, jnp.bfloat16
MESH = pl.DeviceIdType.MESH


def flat_rows(block):
    n, rows, width = block.shape
    if rows % 16:
        return block.astype(f32).reshape(n * rows, width).astype(bf16)
    return block.reshape(n * rows, width)


def to_column(row):
    return jnp.transpose(jnp.broadcast_to(row, (128, row.shape[1])))[:, :1]


def merge(parts):
    peak = functools.reduce(jnp.maximum, [part[0:1] for part in parts])
    total = sum(part[1:2] * jnp.exp(part[0:1] - peak) for part in parts)
    chosen = sum(part[2:3] for part in parts)
    return jnp.concatenate([peak, total, chosen, jnp.zeros_like(peak)], axis=0)


def kernel(
    nA, nB, nC,
    hidden, weight, targets, token_weight,
    loss_out, grad_out,
    H, W, acc, dl, Pb, Sib, x1b, x1r, y1b, y1r, x2b, x2r, y2b, y2r, zb, zr, keep, stb, st,
    wsem, hsem, gz, gx1, gy1, gx2, gy2, gs, rs, rx1, ry1, rx2, ry2, rz, ssem,
):
    rows, cols = hidden.shape
    half = cols // 2
    lo, hi = pl.ds(0, half), pl.ds(half, half)
    p, t = lax.axis_index("pipe"), lax.axis_index("tensor")
    a, c = p // 2, lax.rem(p, 2)
    b, z = lax.rem(t, nB), t // nB

    def at(a_=None, b_=None, z_=None, c_=None):
        a_, b_ = (a if a_ is None else a_), (b if b_ is None else b_)
        z_, c_ = (z if z_ is None else z_), (c if c_ is None else c_)
        return {"pipe": a_ * 2 + c_, "tensor": z_ * nB + b_}

    As = [lax.rem(a + o, nA) for o in range(1, nA)]
    Bs = [lax.rem(b + o, nB) for o in range(1, nB)]
    Zs = [lax.rem(z - o + nC, nC) for o in range(1, nC)]
    sib = at(c_=1 - c)
    peers = [sib] + [at(a_=i) for i in As] + [at(b_=i) for i in Bs] + [at(z_=i) for i in Zs]

    def put(src, dst, sems, here, there, dev):
        pltpu.make_async_remote_copy(
            src_ref=src, dst_ref=dst, send_sem=sems[0].at[here], recv_sem=sems[1].at[there],
            device_id=dev, device_id_type=MESH,
        ).start()

    def got(dst, sems, there):
        pltpu.make_async_remote_copy(
            src_ref=dst, dst_ref=dst, send_sem=sems[0].at[there], recv_sem=sems[1].at[there],
            device_id=sib, device_id_type=MESH,
        ).wait_recv()

    def sent(src, sems, here):
        pltpu.make_async_remote_copy(
            src_ref=src, dst_ref=src, send_sem=sems[0].at[here], recv_sem=sems[1].at[here],
            device_id=sib, device_id_type=MESH,
        ).wait_send()

    wcopy = pltpu.make_async_copy(weight, W, wsem)
    wcopy.start()
    hcopy = pltpu.make_async_copy(hidden, H.at[t, p], hsem)
    hcopy.start()
    barrier = pltpu.get_barrier_semaphore()
    for dev in peers:
        pl.semaphore_signal(barrier, inc=1, device_id=dev, device_id_type=MESH)
    pl.semaphore_wait(barrier, len(peers))

    def slot(k, b_, a_, c_=None):
        return H.at[k * nB + b_, a_ * 2 + (c if c_ is None else c_)]

    for k in Zs:
        put(hidden, slot(z, b, a), gz, k, z, at(z_=k))
    hcopy.wait()
    acc[...] = jnp.zeros_like(acc)

    def spread(i):
        k = lax.rem(z + i, nC)

        @pl.when(i > 0)
        def _():
            got(slot(k, b, a), gz, k)

        own = slot(k, b, a)
        for j in As:
            put(own, own, gx1, (k, j), (k, a), at(a_=j))
        for j in Bs:
            put(own, own, gy1, (k, j), (k, b), at(b_=j))
        put(own, own, gs, (k, b, a), (k, b, a), sib)

    def forward(i):
        k = lax.rem(z + i, nC)
        for j in As:
            blk = slot(k, b, j)
            got(blk, gx1, (k, j))
            for m in Bs:
                put(blk.at[:, lo], blk.at[:, lo], gy2, (k, m, j), (k, b, j), at(b_=m))
        for j in Bs:
            blk = slot(k, j, a)
            got(blk, gy1, (k, j))
            for m in As:
                put(blk.at[:, hi], blk.at[:, hi], gx2, (k, j, m), (k, j, a), at(a_=m))
        for j in As:
            blk = slot(k, b, j)
            put(blk, blk, gs, (k, b, j), (k, b, j), sib)
        for j in Bs:
            blk = slot(k, j, a)
            put(blk, blk, gs, (k, j, a), (k, j, a), sib)

    def finish(i):
        k = lax.rem(z + i, nC)
        for j in As:
            for m in Bs:
                blk = slot(k, m, j)
                got(blk.at[:, lo], gy2, (k, m, j))
                got(blk.at[:, hi], gx2, (k, m, j))
                put(blk, blk, gs, (k, m, j), (k, m, j), sib)

    def multiply(i):
        k = lax.rem(z + i, nC)
        for b_ in range(nB):
            for a_ in range(nA):
                got(slot(k, b_, a_, 1 - c), gs, (k, b_, a_))
        for b_ in range(nB):
            tt = k * nB + b_
            acc[...] += jnp.dot(flat_rows(H[tt]), W[tt], preferred_element_type=f32)

    spread(0)

    def gather_step(i, carry):
        @pl.when(i < nC)
        def _():
            forward(i)

        @pl.when(i < nC - 1)
        def _():
            spread(i + 1)

        @pl.when(i == 1)
        def _():
            wcopy.wait()

        @pl.when(i > 0)
        def _():
            finish(i - 1)
            multiply(i - 1)

        return carry

    lax.fori_loop(0, nC + 1, gather_step, 0)

    logits = acc[...]
    tokens, width = logits.shape
    device_block = p * lax.axis_size("tensor") + t
    target_col = to_column(targets[...].astype(f32)).astype(jnp.int32)
    columns = device_block * width + lax.broadcasted_iota(jnp.int32, (tokens, width), 1)
    hit = target_col == columns
    peak = jnp.max(logits, axis=1, keepdims=True)
    total = jnp.sum(jnp.exp(logits - peak), axis=1, keepdims=True)
    chosen = jnp.sum(jnp.where(hit, logits, 0.0), axis=1, keepdims=True)
    lane = lax.broadcasted_iota(jnp.int32, (tokens, 128), 1)
    packed = jnp.where(lane == 0, peak, jnp.where(lane == 1, total, jnp.where(lane == 2, chosen, 0.0)))
    cur = jnp.transpose(packed)[0:4]
    offset = 0
    for group, me, name in (([1 - c], c, "c_"), (Bs, b, "b_"), (As, a, "a_"), (Zs, z, "z_")):
        size = len(group) + 1
        stage = {"c_": 0, "b_": 1, "a_": 2, "z_": 3}[name]
        stb[stage] = cur
        for j in group:
            put(stb.at[stage], st.at[offset + me], ssem, offset + j, offset + me, at(**{name: j}))
        for j in group:
            got(st.at[offset + j], ssem, offset + j)
        cur = merge([cur] + [st[offset + j] for j in group])
        for j in group:
            sent(stb.at[stage], ssem, offset + j)
        offset += size
    log_total = cur[0:1] + jnp.log(cur[1:2])
    loss_out[...] = log_total - cur[2:3]
    softmax = jnp.exp(acc[...] - to_column(log_total))
    scale = loss_scale * to_column(token_weight[...])
    dl[...] = (scale * (softmax - hit.astype(f32))).astype(bf16)

    def order(i):
        return lax.rem(z + 1 + i, nC)

    def produce(i):
        k = order(i)
        for b_ in range(nB):
            tt = k * nB + b_
            for part in (lo, hi):
                term = lax.dot_general(
                    dl[...], W[tt, part, :], (((1,), (1,)), ((), ())), preferred_element_type=f32
                )
                Pb[tt, :, :, :, part] = term.reshape(nA, 2, rows, half)
            put(Pb.at[tt, :, 1 - c], Sib.at[tt], rs, tt, tt, sib)

    def stage1(i):
        k = order(i)
        for b_ in range(nB):
            tt = k * nB + b_
            got(Sib.at[tt], rs, tt)
            for a_ in range(nA):
                Sib[tt, a_] = Sib[tt, a_] + Pb[tt, a_, c]
        for j in As:
            for b_ in range(nB):
                x1b[k, j, b_] = Sib[k * nB + b_, j, :, lo].astype(bf16)
            put(x1b.at[k, j], x1r.at[k, a], rx1, (k, j), (k, a), at(a_=j))
        for j in Bs:
            for a_ in range(nA):
                y1b[k, j, a_] = Sib[k * nB + j, a_, :, hi].astype(bf16)
            put(y1b.at[k, j], y1r.at[k, b], ry1, (k, j), (k, b), at(b_=j))

    def stage2(i):
        k = order(i)
        for j in As:
            got(x1r.at[k, j], rx1, (k, j))
        for j in Bs:
            y2b[k, j] = (Sib[k * nB + j, a, :, lo] + sum(x1r[k, m, j].astype(f32) for m in As)).astype(bf16)
            put(y2b.at[k, j], y2r.at[k, b], ry2, (k, j), (k, b), at(b_=j))
        keep[:, lo] = Sib[k * nB + b, a, :, lo] + sum(x1r[k, m, b].astype(f32) for m in As)
        for j in Bs:
            got(y1r.at[k, j], ry1, (k, j))
        for j in As:
            x2b[k, j] = (Sib[k * nB + b, j, :, hi] + sum(y1r[k, m, j].astype(f32) for m in Bs)).astype(bf16)
            put(x2b.at[k, j], x2r.at[k, a], rx2, (k, j), (k, a), at(a_=j))
        keep[:, hi] = Sib[k * nB + b, a, :, hi] + sum(y1r[k, m, a].astype(f32) for m in Bs)
        Sib[k * nB + b, a] = keep[...]

    def stage3(i):
        k = order(i)
        for j in Bs:
            got(y2r.at[k, j], ry2, (k, j))
        for j in As:
            got(x2r.at[k, j], rx2, (k, j))
        keep[:, lo] = Sib[k * nB + b, a, :, lo] + sum(y2r[k, j].astype(f32) for j in Bs)
        keep[:, hi] = Sib[k * nB + b, a, :, hi] + sum(x2r[k, j].astype(f32) for j in As)

        @pl.when(i < nC - 1)
        def _():
            zb[k] = keep[...].astype(bf16)
            put(zb.at[k], zr.at[z], rz, k, z, at(z_=k))

    def reduce_step(i, carry):
        @pl.when(i < nC)
        def _():
            produce(i)

        @pl.when((i > 0) & (i < nC + 1))
        def _():
            stage1(i - 1)

        @pl.when((i > 1) & (i < nC + 2))
        def _():
            stage2(i - 2)

        @pl.when(i > 2)
        def _():
            stage3(i - 3)

        return carry

    lax.fori_loop(0, nC + 3, reduce_step, 0)
    for k in Zs:
        got(zr.at[k], rz, k)
    grad_out[...] = keep[...] + sum(zr[k].astype(f32) for k in Zs)

    for k in Zs:
        sent(hidden, gz, k)
        sent(zb.at[k], rz, k)

    def drain(k, carry):
        own = slot(k, b, a)
        for j in As:
            sent(own, gx1, (k, j))
            sent(x1b.at[k, j], rx1, (k, j))
            sent(x2b.at[k, j], rx2, (k, j))
        for j in Bs:
            sent(own, gy1, (k, j))
            sent(y1b.at[k, j], ry1, (k, j))
            sent(y2b.at[k, j], ry2, (k, j))
            for m in As:
                sent(own.at[:, lo], gy2, (k, j, m))
                sent(own.at[:, hi], gx2, (k, j, m))
        for b_ in range(nB):
            for a_ in range(nA):
                sent(own, gs, (k, b_, a_))
            sent(Sib.at[k * nB + b_], rs, k * nB + b_)
        return carry

    lax.fori_loop(0, nC, drain, 0)


def local(hidden, weight, targets, token_weight):
    rows, cols = hidden.shape
    n_pipe, n_tensor = lax.axis_size("pipe"), lax.axis_size("tensor")
    nA, nB, nC = n_pipe // 2, 2, n_tensor // 2
    tokens, width = targets.shape[0], weight.shape[1]
    half = cols // 2
    vmem, dma = pltpu.VMEM, pltpu.SemaphoreType.DMA
    sems = lambda *shape: [dma(shape), dma(shape)]
    groups = 2 + nA + nB + nC
    loss_rows, hidden_grad = pl.pallas_call(
        functools.partial(kernel, nA, nB, nC),
        out_shape=(
            jax.ShapeDtypeStruct((1, tokens), f32),
            jax.ShapeDtypeStruct((rows, cols), f32),
        ),
        in_specs=[
            pl.BlockSpec(memory_space=pl.ANY),
            pl.BlockSpec(memory_space=pl.ANY),
            pl.BlockSpec(memory_space=vmem),
            pl.BlockSpec(memory_space=vmem),
        ],
        out_specs=[pl.BlockSpec(memory_space=vmem)] * 2,
        scratch_shapes=[
            vmem((n_tensor, n_pipe, rows, cols), bf16),
            vmem((n_tensor, cols, width), bf16),
            vmem((tokens, width), f32),
            vmem((tokens, width), bf16),
            vmem((n_tensor, nA, 2, rows, cols), f32),
            vmem((n_tensor, nA, rows, cols), f32),
            vmem((nC, nA, nB, rows, half), bf16),
            vmem((nC, nA, nB, rows, half), bf16),
            vmem((nC, nB, nA, rows, half), bf16),
            vmem((nC, nB, nA, rows, half), bf16),
            vmem((nC, nA, rows, half), bf16),
            vmem((nC, nA, rows, half), bf16),
            vmem((nC, nB, rows, half), bf16),
            vmem((nC, nB, rows, half), bf16),
            vmem((nC, rows, cols), bf16),
            vmem((nC, rows, cols), bf16),
            vmem((rows, cols), f32),
            vmem((4, 4, tokens), f32),
            vmem((groups, 4, tokens), f32),
            dma,
            dma,
            sems(nC),
            sems(nC, nA),
            sems(nC, nB),
            sems(nC, nB, nA),
            sems(nC, nB, nA),
            sems(nC, nB, nA),
            sems(n_tensor),
            sems(nC, nA),
            sems(nC, nB),
            sems(nC, nA),
            sems(nC, nB),
            sems(nC),
            sems(groups),
        ],
        compiler_params=pltpu.CompilerParams(
            collective_id=0, has_side_effects=True, vmem_limit_bytes=62 * 1024 * 1024
        ),
    )(
        hidden,
        weight.reshape(n_tensor, cols, width),
        targets.reshape(1, tokens),
        token_weight.reshape(1, tokens),
    )
    token_loss = lax.dynamic_slice_in_dim(loss_rows[0], lax.axis_index("pipe") * rows, rows, 0)
    return token_loss, hidden_grad


def solution(mesh):
    in_specs = (P("pipe", "tensor"), P(None, ("pipe", "tensor")), P(), P())
    out_specs = (P("pipe"), P("pipe", "tensor"))
    return jax.shard_map(local, mesh=mesh, in_specs=in_specs, out_specs=out_specs, check_vma=False)
```

time: 390 us -> 99.8 us (0.26)
  waiting for transfers between devices: 273 us -> 0 us
  Pallas kernels: 0 us -> 93.4 us
  blocking collectives: 80.3 us -> 0 us
  matrix products: 20 us -> 0 us
  between operations: 13.8 us -> 0.64 us
  local copies, waits for them, and re-layouts: 0.59 us -> 5.53 us
    reduce_scatter x2 -> x0, waiting for transfers between devices: 178 us -> none  [the longest x1 99.5 us: local(): lax.psum_scatter(lax.dot_general(dlogits, weight, (((1,), (1,)), ((), ())...]
    all_gather x2 -> x0, waiting for transfers between devices: 94.7 us -> none  [the longest x1 49.2 us: local(): full_rows = lax.all_gather(hidden, 'tensor', axis=1, tiled=True)]
    pallas_call x0 -> x1, Pallas kernels: none -> 93.4 us  [local(): pl.pallas_call(functools.partial(kernel, nA, nB, nC), out_shape=(jax.Shap...]
    psum x1 -> x0, blocking collectives: 41 us -> none  [local(): lax.psum((local_total, chosen), ('pipe', 'tensor'))]
    pmax x1 -> x0, blocking collectives: 39.3 us -> none  [local(): global_peak = lax.pmax(local_peak, ('pipe', 'tensor'))]
    dot_general x2 -> x0, matrix products: 20 us -> none  [the longest x1 12 us: local(): lax.dot_general(dlogits, weight, (((1,), (1,)), ((), ())), preferred_elem...]
  transfers between devices with their start and end apart: 4 -> 0, of which waited for: 4 -> 0; matrix products, arithmetic and copies ran while one was open for 0% -> 0% of each run, Pallas kernels for 0% -> 0%
where the time goes in v1:
time: 99.8 us; the launch traced here: 99.5 us
  Pallas kernels  93.4 us (94%)
  local copies, waits for them, and re-layouts  5.53 us (6%)
    pallas_call x1, Pallas kernels, local(): pl.pallas_call(functools.partial(kernel, nA, nB, nC), out_shape=(jax.Shap...  93.4 us

profile of v1, /device:TPU:0, one launch (start us, length us, event | category | flops | bytes accessed | tf_op | source)
XLA Modules:
  0.0 99.5 jit_solution(8075000122496242131)
XLA Ops:
  0.6 1.2 %reshape.15.targets = s32[1,384]{1,0:T(1,128)} reshape(s32[384]{0:T(512)} %param.6) | data formatting | bytes 3072 | tf_op jit(solution)/shard_map/reshape | solution.py:373
  1.9 1.2 %reshape.16.token_weight = f32[1,384]{1,0:T(1,128)} reshape(f32[384]{0:T(512)} %param.7) | data formatting | bytes 3072 | tf_op jit(solution)/shard_map/reshape | solution.py:374
  3.1 93.4 %shard_map.59 = (f32[1,384]{1,0:T(1,128)}, f32[96,1024]{1,0:T(8,128)}) custom-call(bf16[96,1024]{1,0:T(8,128)(2,1)} %hidden.1, bf16[8,1024,512]{2,1,0:T(8,128)(2,1)} %bitcast.3, s32[1,384]{1,0:T(1,128)} %reshape.15.targets, f32[1,384]{1,0:T(1,128)} %reshape.16.token_weight), custom_call_target="tpu_custom_call" | custom-call | tf_op jit(solution)/shard_map/pallas_call | solution.py:318
  96.5 1.3 %dynamic-slice_bitcast_fusion = f32[96]{0:T(128)} fusion(f32[1,384]{1,0:T(1,128)} %get-tuple-element.4, s32[]{:T(128)S(6)} %select_n.3), kind=kLoop, calls=%fused_computation | loop fusion | bytes 772 | tf_op jit(solution)/shard_map/dynamic_slice | solution.py:376
  97.8 1.8 %copy.7 = f32[96,1024]{1,0:T(8,128)} copy(f32[96,1024]{1,0:T(8,128)} %get-tuple-element.9) | data formatting | bytes 786432

commit v2 on v1

--- a/solution.py
+++ b/solution.py
@@ -53,7 +53,11 @@
     Bs = [lax.rem(b + o, nB) for o in range(1, nB)]
     Zs = [lax.rem(z - o + nC, nC) for o in range(1, nC)]
     sib = at(c_=1 - c)
-    peers = [sib] + [at(a_=i) for i in As] + [at(b_=i) for i in Bs] + [at(z_=i) for i in Zs]
+    Plane = [
+        ((a_ * nB + b_) * 2 + c_, at(a_=a_, b_=b_, c_=c_))
+        for a_ in [a] + As for b_ in [b] + Bs for c_ in (c, 1 - c)
+    ][1:]
+    peers = [dev for _, dev in Plane] + [at(z_=i) for i in Zs]
 
     def put(src, dst, sems, here, there, dev):
         pltpu.make_async_remote_copy(
@@ -85,19 +89,33 @@
     def slot(k, b_, a_, c_=None):
         return H.at[k * nB + b_, a_ * 2 + (c if c_ is None else c_)]
 
-    for k in Zs:
-        put(hidden, slot(z, b, a), gz, k, z, at(z_=k))
     hcopy.wait()
     acc[...] = jnp.zeros_like(acc)
+    left, right = z, nC - 1 - z
+    both = jnp.minimum(left, right)
+    longer = jnp.where(left > right, -1, 1)
+
+    def nearest(i):
+        d = (i + 1) // 2
+        turn = jnp.where(lax.rem(i, 2) == 1, -d, d)
+        return z + jnp.where(i <= 2 * both, turn, longer * (i - both))
 
     def spread(i):
-        k = lax.rem(z + i, nC)
-
-        @pl.when(i > 0)
-        def _():
-            got(slot(k, b, a), gz, k)
-
+        k = nearest(i)
         own = slot(k, b, a)
+
+        @pl.when(k != z)
+        def _():
+            got(own, gz, (k, 0))
+
+        @pl.when((k <= z) & (z < nC - 1))
+        def _():
+            put(own, own, gz, (k, 1), (k, 0), at(z_=z + 1))
+
+        @pl.when((k >= z) & (z > 0))
+        def _():
+            put(own, own, gz, (k, 0), (k, 0), at(z_=z - 1))
+
         for j in As:
             put(own, own, gx1, (k, j), (k, a), at(a_=j))
         for j in Bs:
@@ -105,7 +123,7 @@
         put(own, own, gs, (k, b, a), (k, b, a), sib)
 
     def forward(i):
-        k = lax.rem(z + i, nC)
+        k = nearest(i)
         for j in As:
             blk = slot(k, b, j)
             got(blk, gx1, (k, j))
@@ -124,7 +142,7 @@
             put(blk, blk, gs, (k, j, a), (k, j, a), sib)
 
     def finish(i):
-        k = lax.rem(z + i, nC)
+        k = nearest(i)
         for j in As:
             for m in Bs:
                 blk = slot(k, m, j)
@@ -133,7 +151,7 @@
                 put(blk, blk, gs, (k, m, j), (k, m, j), sib)
 
     def multiply(i):
-        k = lax.rem(z + i, nC)
+        k = nearest(i)
         for b_ in range(nB):
             for a_ in range(nA):
                 got(slot(k, b_, a_, 1 - c), gs, (k, b_, a_))
@@ -144,31 +162,31 @@
     spread(0)
 
     def gather_step(i, carry):
+        @pl.when(i < nC - 1)
+        def _():
+            spread(i + 1)
+
         @pl.when(i < nC)
         def _():
             forward(i)
 
-        @pl.when(i < nC - 1)
-        def _():
-            spread(i + 1)
-
-        @pl.when(i == 1)
+        @pl.when(i == 2)
         def _():
             wcopy.wait()
 
-        @pl.when(i > 0)
-        def _():
-            finish(i - 1)
-            multiply(i - 1)
+        @pl.when(i > 1)
+        def _():
+            finish(i - 2)
+            multiply(i - 2)
 
         return carry
 
-    lax.fori_loop(0, nC + 1, gather_step, 0)
+    lax.fori_loop(0, nC + 2, gather_step, 0)
 
     logits = acc[...]
     tokens, width = logits.shape
     device_block = p * lax.axis_size("tensor") + t
-    target_col = to_column(targets[...].astype(f32)).astype(jnp.int32)
+    target_col = to_column(targets[...].reshape(1, tokens).astype(f32)).astype(jnp.int32)
     columns = device_block * width + lax.broadcasted_iota(jnp.int32, (tokens, width), 1)
     hit = target_col == columns
     peak = jnp.max(logits, axis=1, keepdims=True)
@@ -177,23 +195,22 @@
     lane = lax.broadcasted_iota(jnp.int32, (tokens, 128), 1)
     packed = jnp.where(lane == 0, peak, jnp.where(lane == 1, total, jnp.where(lane == 2, chosen, 0.0)))
     cur = jnp.transpose(packed)[0:4]
-    offset = 0
-    for group, me, name in (([1 - c], c, "c_"), (Bs, b, "b_"), (As, a, "a_"), (Zs, z, "z_")):
-        size = len(group) + 1
-        stage = {"c_": 0, "b_": 1, "a_": 2, "z_": 3}[name]
+    plane = nA * nB * 2
+    here = (a * nB + b) * 2 + c
+    for stage, group, base, me in ((0, Plane, 0, here), (1, [(k, at(z_=k)) for k in Zs], plane, z)):
         stb[stage] = cur
-        for j in group:
-            put(stb.at[stage], st.at[offset + me], ssem, offset + j, offset + me, at(**{name: j}))
-        for j in group:
-            got(st.at[offset + j], ssem, offset + j)
-        cur = merge([cur] + [st[offset + j] for j in group])
-        for j in group:
-            sent(stb.at[stage], ssem, offset + j)
-        offset += size
+        for j, dev in group:
+            put(stb.at[stage], st.at[base + me], ssem, base + j, base + me, dev)
+        for j, _ in group:
+            got(st.at[base + j], ssem, base + j)
+        cur = merge([cur] + [st[base + j] for j, _ in group])
+        for j, _ in group:
+            sent(stb.at[stage], ssem, base + j)
     log_total = cur[0:1] + jnp.log(cur[1:2])
-    loss_out[...] = log_total - cur[2:3]
+    loss = jnp.broadcast_to(log_total - cur[2:3], (8, tokens))
+    loss_out[...] = pltpu.roll(loss, lax.rem(tokens - p * rows, tokens), axis=1)[0, :rows]
     softmax = jnp.exp(acc[...] - to_column(log_total))
-    scale = loss_scale * to_column(token_weight[...])
+    scale = loss_scale * to_column(token_weight[...].reshape(1, tokens))
     dl[...] = (scale * (softmax - hit.astype(f32))).astype(bf16)
 
     def order(i):
@@ -281,11 +298,19 @@
     grad_out[...] = keep[...] + sum(zr[k].astype(f32) for k in Zs)
 
     for k in Zs:
-        sent(hidden, gz, k)
         sent(zb.at[k], rz, k)
 
     def drain(k, carry):
         own = slot(k, b, a)
+
+        @pl.when((k <= z) & (z < nC - 1))
+        def _():
+            sent(own, gz, (k, 1))
+
+        @pl.when((k >= z) & (z > 0))
+        def _():
+            sent(own, gz, (k, 0))
+
         for j in As:
             sent(own, gx1, (k, j))
             sent(x1b.at[k, j], rx1, (k, j))
@@ -314,11 +339,11 @@
     half = cols // 2
     vmem, dma = pltpu.VMEM, pltpu.SemaphoreType.DMA
     sems = lambda *shape: [dma(shape), dma(shape)]
-    groups = 2 + nA + nB + nC
-    loss_rows, hidden_grad = pl.pallas_call(
+    groups = 2 * nA * nB + nC
+    token_loss, hidden_grad = pl.pallas_call(
         functools.partial(kernel, nA, nB, nC),
         out_shape=(
-            jax.ShapeDtypeStruct((1, tokens), f32),
+            jax.ShapeDtypeStruct((rows,), f32),
             jax.ShapeDtypeStruct((rows, cols), f32),
         ),
         in_specs=[
@@ -346,11 +371,11 @@
             vmem((nC, rows, cols), bf16),
             vmem((nC, rows, cols), bf16),
             vmem((rows, cols), f32),
-            vmem((4, 4, tokens), f32),
+            vmem((2, 4, tokens), f32),
             vmem((groups, 4, tokens), f32),
             dma,
             dma,
-            sems(nC),
+            sems(nC, 2),
             sems(nC, nA),
             sems(nC, nB),
             sems(nC, nB, nA),
@@ -370,10 +395,9 @@
     )(
         hidden,
         weight.reshape(n_tensor, cols, width),
-        targets.reshape(1, tokens),
-        token_weight.reshape(1, tokens),
+        targets,
+        token_weight,
     )
-    token_loss = lax.dynamic_slice_in_dim(loss_rows[0], lax.axis_index("pipe") * rows, rows, 0)
     return token_loss, hidden_grad
 
 

time: 99.8 us -> 90.6 us (0.908)
  Pallas kernels: 93.4 us -> 86.9 us
  local copies, waits for them, and re-layouts: 5.53 us -> 2.89 us
    pallas_call x1, Pallas kernels: 93.4 us -> 86.9 us  [local(): pl.pallas_call(functools.partial(kernel, nA, nB, nC), out_shape=(jax.Shap...]
    reshape x2 -> x0, local copies, waits for them, and re-layouts: 2.49 us -> none  [the longest x1 1.25 us: local(): targets.reshape(1, tokens)]
    dynamic_slice x1 -> x0, local copies, waits for them, and re-layouts: 1.27 us -> none  [local(): lax.dynamic_slice_in_dim(loss_rows[0], lax.axis_index('pipe') * rows, row...]
    unnamed x1 -> x2, local copies, waits for them, and re-layouts: 1.77 us -> 2.89 us
where the time goes in v2:
time: 90.6 us; the launch traced here: 90.4 us
  Pallas kernels  86.9 us (96%)
  local copies, waits for them, and re-layouts  2.89 us (3%)
    pallas_call x1, Pallas kernels, local(): pl.pallas_call(functools.partial(kernel, nA, nB, nC), out_shape=(jax.Shap...  86.9 us
    unnamed x2, local copies, waits for them, and re-layouts  2.89 us

profile of v2, /device:TPU:0, one launch (start us, length us, event | category | flops | bytes accessed | tf_op | source)
XLA Modules:
  0.0 90.4 jit_solution(1825220981430426262)
XLA Ops:
  0.6 86.9 %shard_map.59 = (f32[96]{0:T(128)}, f32[96,1024]{1,0:T(8,128)}) custom-call(bf16[96,1024]{1,0:T(8,128)(2,1)} %hidden.1, bf16[8,1024,512]{2,1,0:T(8,128)(2,1)} %bitcast.1, s32[384]{0:T(512)} %targets.1, f32[384]{0:T(512)} %token_weight.1), custom_call_target="tpu_custom_call" | custom-call | tf_op jit(solution)/shard_map/pallas_call | solution.py:343
  87.5 1.1 %copy.8 = f32[96]{0:T(128)} copy(f32[96]{0:T(128)} %get-tuple-element.4) | data formatting | bytes 768
  88.6 1.8 %copy.9 = f32[96,1024]{1,0:T(8,128)} copy(f32[96,1024]{1,0:T(8,128)} %get-tuple-element.5) | data formatting | bytes 786432

commit v3 on v0

v3 whole, which is shorter than its diff:
```python
import functools

import jax
import jax.numpy as jnp
from jax import lax
from jax.experimental import pallas as pl
from jax.experimental.pallas import tpu as pltpu
from jax.sharding import PartitionSpec as P

loss_scale = 32.0
f32, bf16 = jnp.float32, jnp.bfloat16
MESH = pl.DeviceIdType.MESH


def flat_rows(block):
    n, rows, width = block.shape
    if rows % 16:
        return block.astype(f32).reshape(n * rows, width).astype(bf16)
    return block.reshape(n * rows, width)


def to_column(row):
    return jnp.transpose(jnp.broadcast_to(row, (128, row.shape[1])))[:, :1]


def merge(parts):
    peak = functools.reduce(jnp.maximum, [part[0:1] for part in parts])
    total = sum(part[1:2] * jnp.exp(part[0:1] - peak) for part in parts)
    chosen = sum(part[2:3] for part in parts)
    return jnp.concatenate([peak, total, chosen, jnp.zeros_like(peak)], axis=0)


def kernel(
    nA, nB, nC, nH,
    hidden, weight, targets, token_weight,
    loss_out, grad_out,
    H, W, acc, dl, Pb, Sib, x1b, x1r, y1b, y1r, x2b, x2r, y2b, y2r, zb, zr, keep, stb, st, lossb,
    wsem, hsem, gz, gx1, gy1, gx2, gy2, gs, rs, rx1, ry1, rx2, ry2, rz, ssem,
):
    rows, cols = hidden.shape
    chunk = rows // nH
    half = cols // 2
    lo, hi = pl.ds(0, half), pl.ds(half, half)
    p, t = lax.axis_index("pipe"), lax.axis_index("tensor")
    a, c = p // 2, lax.rem(p, 2)
    b, z = lax.rem(t, nB), t // nB

    def at(a_=None, b_=None, z_=None, c_=None):
        a_, b_ = (a if a_ is None else a_), (b if b_ is None else b_)
        z_, c_ = (z if z_ is None else z_), (c if c_ is None else c_)
        return {"pipe": a_ * 2 + c_, "tensor": z_ * nB + b_}

    As = [lax.rem(a + o, nA) for o in range(1, nA)]
    Bs = [lax.rem(b + o, nB) for o in range(1, nB)]
    Zs = [lax.rem(z - o + nC, nC) for o in range(1, nC)]
    sib = at(c_=1 - c)
    Plane = [
        ((a_ * nB + b_) * 2 + c_, at(a_=a_, b_=b_, c_=c_))
        for a_ in [a] + As for b_ in [b] + Bs for c_ in (c, 1 - c)
    ][1:]
    peers = [dev for _, dev in Plane] + [at(z_=i) for i in Zs]

    def put(src, dst, sems, here, there, dev):
        pltpu.make_async_remote_copy(
            src_ref=src, dst_ref=dst, send_sem=sems[0].at[here], recv_sem=sems[1].at[there],
            device_id=dev, device_id_type=MESH,
        ).start()

    def got(dst, sems, there):
        pltpu.make_async_remote_copy(
            src_ref=dst, dst_ref=dst, send_sem=sems[0].at[there], recv_sem=sems[1].at[there],
            device_id=sib, device_id_type=MESH,
        ).wait_recv()

    def sent(src, sems, here):
        pltpu.make_async_remote_copy(
            src_ref=src, dst_ref=src, send_sem=sems[0].at[here], recv_sem=sems[1].at[here],
            device_id=sib, device_id_type=MESH,
        ).wait_send()

    wcopy = pltpu.make_async_copy(weight, W, wsem)
    hcopies = [
        pltpu.make_async_copy(hidden.at[pl.ds(h * chunk, chunk)], H.at[h, t, p], hsem.at[h])
        for h in range(nH)
    ]
    for copy in hcopies:
        copy.start()
    wcopy.start()
    barrier = pltpu.get_barrier_semaphore()
    for dev in peers:
        pl.semaphore_signal(barrier, inc=1, device_id=dev, device_id_type=MESH)
    for copy in hcopies:
        copy.wait()
    acc[...] = jnp.zeros_like(acc)
    target_col = to_column(targets[...].reshape(1, -1).astype(f32)).astype(jnp.int32)
    scale_col = loss_scale * to_column(token_weight[...].reshape(1, -1))
    pl.semaphore_wait(barrier, len(peers))

    def slot(h, k, b_, a_, c_=None):
        return H.at[h, k * nB + b_, a_ * 2 + (c if c_ is None else c_)]

    left, right = z, nC - 1 - z
    both = jnp.minimum(left, right)
    longer = jnp.where(left > right, -1, 1)

    def nearest(step):
        h, i = step // nC, lax.rem(step, nC)
        d = (i + 1) // 2
        turn = jnp.where(lax.rem(i, 2) == 1, -d, d)
        return h, z + jnp.where(i <= 2 * both, turn, longer * (i - both))

    def spread(step):
        h, k = nearest(step)
        own = slot(h, k, b, a)

        @pl.when(k != z)
        def _():
            got(own, gz, (h, k, 0))

        @pl.when((k <= z) & (z < nC - 1))
        def _():
            put(own, own, gz, (h, k, 1), (h, k, 0), at(z_=z + 1))

        @pl.when((k >= z) & (z > 0))
        def _():
            put(own, own, gz, (h, k, 0), (h, k, 0), at(z_=z - 1))

        for j in As:
            put(own, own, gx1, (h, k, j), (h, k, a), at(a_=j))
        for j in Bs:
            put(own, own, gy1, (h, k, j), (h, k, b), at(b_=j))
        put(own, own, gs, (h, k, b, a), (h, k, b, a), sib)

    def forward(step):
        h, k = nearest(step)
        for j in As:
            blk = slot(h, k, b, j)
            got(blk, gx1, (h, k, j))
            for m in Bs:
                put(blk.at[:, lo], blk.at[:, lo], gy2, (h, k, m, j), (h, k, b, j), at(b_=m))
        for j in Bs:
            blk = slot(h, k, j, a)
            got(blk, gy1, (h, k, j))
            for m in As:
                put(blk.at[:, hi], blk.at[:, hi], gx2, (h, k, j, m), (h, k, j, a), at(a_=m))
        for j in As:
            blk = slot(h, k, b, j)
            put(blk, blk, gs, (h, k, b, j), (h, k, b, j), sib)
        for j in Bs:
            blk = slot(h, k, j, a)
            put(blk, blk, gs, (h, k, j, a), (h, k, j, a), sib)

    def finish(step):
        h, k = nearest(step)
        for j in As:
            for m in Bs:
                blk = slot(h, k, m, j)
                got(blk.at[:, lo], gy2, (h, k, m, j))
                got(blk.at[:, hi], gx2, (h, k, m, j))
                put(blk, blk, gs, (h, k, m, j), (h, k, m, j), sib)

    def multiply(step):
        h, k = nearest(step)
        for b_ in range(nB):
            for a_ in range(nA):
                got(slot(h, k, b_, a_, 1 - c), gs, (h, k, b_, a_))
        for b_ in range(nB):
            tt = k * nB + b_
            acc[h] += jnp.dot(flat_rows(H[h, tt]), W[tt], preferred_element_type=f32)

    tokens, width = acc.shape[1:]
    padded = stb.shape[-1]
    device_block = p * lax.axis_size("tensor") + t
    plane = nA * nB * 2
    groups = (
        (Plane, 0, (a * nB + b) * 2 + c),
        ([(k, at(z_=k)) for k in Zs], plane, z),
    )

    def of_chunk(column, h):
        sections = nA * 2
        return column.reshape(sections, nH, chunk, 1)[:, h].reshape(sections * chunk, 1)

    def hits(h):
        columns = device_block * width + lax.broadcasted_iota(jnp.int32, (tokens, width), 1)
        return of_chunk(target_col, h) == columns

    def share(h, stage, mine):
        group, base, me = groups[stage]
        stb[h, stage] = mine
        for j, dev in group:
            put(stb.at[h, stage], st.at[h, base + me], ssem, (h, base + j), (h, base + me), dev)

    def merged(h, stage):
        group, base, me = groups[stage]
        for j, _ in group:
            got(st.at[h, base + j], ssem, (h, base + j))
        return merge([stb[h, stage]] + [st[h, base + j] for j, _ in group])

    def stats_local(h):
        logits = acc[h]
        peak = jnp.max(logits, axis=1, keepdims=True)
        total = jnp.sum(jnp.exp(logits - peak), axis=1, keepdims=True)
        chosen = jnp.sum(jnp.where(hits(h), logits, 0.0), axis=1, keepdims=True)
        lane = lax.broadcasted_iota(jnp.int32, (tokens, 128), 1)
        packed = jnp.where(
            lane == 0, peak, jnp.where(lane == 1, total, jnp.where(lane == 2, chosen, 0.0))
        )
        if padded > tokens:
            packed = jnp.concatenate([packed, jnp.zeros((padded - tokens, 128), f32)], axis=0)
        share(h, 0, jnp.transpose(packed)[0:4])

    def stats_plane(h):
        share(h, 1, merged(h, 0))

    def stats_line(h):
        cur = merged(h, 1)
        log_total = cur[0:1] + jnp.log(cur[1:2])
        loss = jnp.broadcast_to(log_total - cur[2:3], (8, padded))
        lossb[h] = pltpu.roll(loss, lax.rem((h - p) * chunk + nA * 2 * padded, padded), axis=1)
        softmax = jnp.exp(acc[h] - to_column(log_total)[:tokens])
        dl[h] = (of_chunk(scale_col, h) * (softmax - hits(h).astype(f32))).astype(bf16)

    def order(step):
        return step // nC, lax.rem(z + 1 + lax.rem(step, nC), nC)

    def produce(step):
        h, k = order(step)
        for b_ in range(nB):
            tt = k * nB + b_
            for part in (lo, hi):
                term = lax.dot_general(
                    dl[h], W[tt, part, :], (((1,), (1,)), ((), ())), preferred_element_type=f32
                )
                Pb[h, tt, :, :, :, part] = term.reshape(nA, 2, chunk, half)
            put(Pb.at[h, tt, :, 1 - c], Sib.at[h, tt], rs, (h, tt), (h, tt), sib)

    def stage1(step):
        h, k = order(step)
        for b_ in range(nB):
            tt = k * nB + b_
            got(Sib.at[h, tt], rs, (h, tt))
            for a_ in range(nA):
                Sib[h, tt, a_] = Sib[h, tt, a_] + Pb[h, tt, a_, c]
        for j in As:
            for b_ in range(nB):
                x1b[h, k, j, b_] = Sib[h, k * nB + b_, j, :, lo].astype(bf16)
            put(x1b.at[h, k, j], x1r.at[h, k, a], rx1, (h, k, j), (h, k, a), at(a_=j))
        for j in Bs:
            for a_ in range(nA):
                y1b[h, k, j, a_] = Sib[h, k * nB + j, a_, :, hi].astype(bf16)
            put(y1b.at[h, k, j], y1r.at[h, k, b], ry1, (h, k, j), (h, k, b), at(b_=j))

    def stage2(step):
        h, k = order(step)
        tb = k * nB + b
        for j in As:
            got(x1r.at[h, k, j], rx1, (h, k, j))
        for j in Bs:
            term = sum(x1r[h, k, m, j].astype(f32) for m in As)
            y2b[h, k, j] = (Sib[h, k * nB + j, a, :, lo] + term).astype(bf16)
            put(y2b.at[h, k, j], y2r.at[h, k, b], ry2, (h, k, j), (h, k, b), at(b_=j))
        for j in Bs:
            got(y1r.at[h, k, j], ry1, (h, k, j))
        for j in As:
            term = sum(y1r[h, k, m, j].astype(f32) for m in Bs)
            x2b[h, k, j] = (Sib[h, tb, j, :, hi] + term).astype(bf16)
            put(x2b.at[h, k, j], x2r.at[h, k, a], rx2, (h, k, j), (h, k, a), at(a_=j))
        Sib[h, tb, a, :, lo] = Sib[h, tb, a, :, lo] + sum(x1r[h, k, m, b].astype(f32) for m in As)
        Sib[h, tb, a, :, hi] = Sib[h, tb, a, :, hi] + sum(y1r[h, k, m, a].astype(f32) for m in Bs)

    def stage3(step):
        h, k = order(step)
        tb = k * nB + b
        for j in Bs:
            got(y2r.at[h, k, j], ry2, (h, k, j))
        for j in As:
            got(x2r.at[h, k, j], rx2, (h, k, j))
        keep[h, :, lo] = Sib[h, tb, a, :, lo] + sum(y2r[h, k, j].astype(f32) for j in Bs)
        keep[h, :, hi] = Sib[h, tb, a, :, hi] + sum(x2r[h, k, j].astype(f32) for j in As)

        @pl.when(lax.rem(step, nC) < nC - 1)
        def _():
            zb[h, k] = keep[h].astype(bf16)
            put(zb.at[h, k], zr.at[h, z], rz, (h, k), (h, z), at(z_=k))

    steps = nH * nC
    offset = nC + 4

    def during(i, first, count, action, lag):
        @pl.when((i >= first + lag) & (i < first + lag + count))
        def _():
            action(i - first - lag)

    def once(i, when, action, h):
        @pl.when(i == when)
        def _():
            action(h)

    spread(0)

    def step(i, carry):
        during(i, 0, steps - 1, lambda n: spread(n + 1), 0)
        during(i, 0, steps, forward, 0)

        @pl.when(i == 2)
        def _():
            wcopy.wait()

        during(i, offset, steps, produce, 0)
        during(i, offset, steps, stage1, 1)
        during(i, offset, steps, stage2, 2)
        during(i, offset, steps, stage3, 3)
        during(i, 0, steps, finish, 2)
        during(i, 0, steps, multiply, 2)
        for h in range(nH):
            once(i, (h + 1) * nC + 1, stats_local, h)
            once(i, (h + 1) * nC + 2, stats_plane, h)
            once(i, (h + 1) * nC + 3, stats_line, h)
        return carry

    lax.fori_loop(0, offset + steps + 3, step, 0)
    lane = lax.broadcasted_iota(jnp.int32, (8, padded), 1)
    loss = lossb[0]
    for h in range(1, nH):
        loss = jnp.where(lane >= h * chunk, lossb[h], loss)
    loss_out[...] = loss[0, :rows]
    for h in range(nH):
        for k in Zs:
            got(zr.at[h, k], rz, (h, k))
        grad_out[pl.ds(h * chunk, chunk), :] = keep[h] + sum(zr[h, k].astype(f32) for k in Zs)

    for h in range(nH):
        for k in Zs:
            sent(zb.at[h, k], rz, (h, k))
        for stage, (group, base, _) in enumerate(groups):
            for j, _ in group:
                sent(stb.at[h, stage], ssem, (h, base + j))

    def drain(n, carry):
        h, k = n // nC, lax.rem(n, nC)
        own = slot(h, k, b, a)

        @pl.when((k <= z) & (z < nC - 1))
        def _():
            sent(own, gz, (h, k, 1))

        @pl.when((k >= z) & (z > 0))
        def _():
            sent(own, gz, (h, k, 0))

        for j in As:
            sent(own, gx1, (h, k, j))
            sent(x1b.at[h, k, j], rx1, (h, k, j))
            sent(x2b.at[h, k, j], rx2, (h, k, j))
        for j in Bs:
            sent(own, gy1, (h, k, j))
            sent(y1b.at[h, k, j], ry1, (h, k, j))
            sent(y2b.at[h, k, j], ry2, (h, k, j))
            for m in As:
                sent(own.at[:, lo], gy2, (h, k, j, m))
                sent(own.at[:, hi], gx2, (h, k, j, m))
        for b_ in range(nB):
            for a_ in range(nA):
                sent(own, gs, (h, k, b_, a_))
            sent(Sib.at[h, k * nB + b_], rs, (h, k * nB + b_))
        return carry

    lax.fori_loop(0, steps, drain, 0)


def local(hidden, weight, targets, token_weight):
    rows, cols = hidden.shape
    n_pipe, n_tensor = lax.axis_size("pipe"), lax.axis_size("tensor")
    nA, nB, nC = n_pipe // 2, 2, n_tensor // 2
    tokens, width = targets.shape[0], weight.shape[1]
    half = cols // 2
    vmem, dma = pltpu.VMEM, pltpu.SemaphoreType.DMA
    sems = lambda *shape: [dma(shape), dma(shape)]
    groups = 2 * nA * nB + nC
    nH = 2 if rows % 32 == 0 else 1
    chunk = rows // nH
    part = n_pipe * chunk
    padded = -(-part // 128) * 128
    token_loss, hidden_grad = pl.pallas_call(
        functools.partial(kernel, nA, nB, nC, nH),
        out_shape=(
            jax.ShapeDtypeStruct((rows,), f32),
            jax.ShapeDtypeStruct((rows, cols), f32),
        ),
        in_specs=[
            pl.BlockSpec(memory_space=pl.ANY),
            pl.BlockSpec(memory_space=pl.ANY),
            pl.BlockSpec(memory_space=vmem),
            pl.BlockSpec(memory_space=vmem),
        ],
        out_specs=[pl.BlockSpec(memory_space=vmem)] * 2,
        scratch_shapes=[
            vmem((nH, n_tensor, n_pipe, chunk, cols), bf16),
            vmem((n_tensor, cols, width), bf16),
            vmem((nH, part, width), f32),
            vmem((nH, part, width), bf16),
            vmem((nH, n_tensor, nA, 2, chunk, cols), f32),
            vmem((nH, n_tensor, nA, chunk, cols), f32),
            vmem((nH, nC, nA, nB, chunk, half), bf16),
            vmem((nH, nC, nA, nB, chunk, half), bf16),
            vmem((nH, nC, nB, nA, chunk, half), bf16),
            vmem((nH, nC, nB, nA, chunk, half), bf16),
            vmem((nH, nC, nA, chunk, half), bf16),
            vmem((nH, nC, nA, chunk, half), bf16),
            vmem((nH, nC, nB, chunk, half), bf16),
            vmem((nH, nC, nB, chunk, half), bf16),
            vmem((nH, nC, chunk, cols), bf16),
            vmem((nH, nC, chunk, cols), bf16),
            vmem((nH, chunk, cols), f32),
            vmem((nH, 2, 4, padded), f32),
            vmem((nH, groups, 4, padded), f32),
            vmem((nH, 8, padded), f32),
            dma,
            dma((nH,)),
            sems(nH, nC, 2),
            sems(nH, nC, nA),
            sems(nH, nC, nB),
            sems(nH, nC, nB, nA),
            sems(nH, nC, nB, nA),
            sems(nH, nC, nB, nA),
            sems(nH, n_tensor),
            sems(nH, nC, nA),
            sems(nH, nC, nB),
            sems(nH, nC, nA),
            sems(nH, nC, nB),
            sems(nH, nC),
            sems(nH, groups),
        ],
        compiler_params=pltpu.CompilerParams(
            collective_id=0, has_side_effects=True, vmem_limit_bytes=62 * 1024 * 1024
        ),
    )(
        hidden,
        weight.reshape(n_tensor, cols, width),
        targets,
        token_weight,
    )
    return token_loss, hidden_grad


def solution(mesh):
    in_specs = (P("pipe", "tensor"), P(None, ("pipe", "tensor")), P(), P())
    out_specs = (P("pipe"), P("pipe", "tensor"))
    return jax.shard_map(local, mesh=mesh, in_specs=in_specs, out_specs=out_specs, check_vma=False)
```

time: 390 us -> 85.5 us (0.22)
  waiting for transfers between devices: 273 us -> 0 us
  Pallas kernels: 0 us -> 81.8 us
  blocking collectives: 80.3 us -> 0 us
  matrix products: 20 us -> 0 us
  between operations: 13.8 us -> 0.64 us
    reduce_scatter x2 -> x0, waiting for transfers between devices: 178 us -> none  [the longest x1 99.5 us: local(): lax.psum_scatter(lax.dot_general(dlogits, weight, (((1,), (1,)), ((), ())...]
    all_gather x2 -> x0, waiting for transfers between devices: 94.7 us -> none  [the longest x1 49.2 us: local(): full_rows = lax.all_gather(hidden, 'tensor', axis=1, tiled=True)]
    pallas_call x0 -> x1, Pallas kernels: none -> 81.8 us  [local(): pl.pallas_call(functools.partial(kernel, nA, nB, nC, nH), out_shape=(jax....]
    psum x1 -> x0, blocking collectives: 41 us -> none  [local(): lax.psum((local_total, chosen), ('pipe', 'tensor'))]
    pmax x1 -> x0, blocking collectives: 39.3 us -> none  [local(): global_peak = lax.pmax(local_peak, ('pipe', 'tensor'))]
    dot_general x2 -> x0, matrix products: 20 us -> none  [the longest x1 12 us: local(): lax.dot_general(dlogits, weight, (((1,), (1,)), ((), ())), preferred_elem...]
  transfers between devices with their start and end apart: 4 -> 0, of which waited for: 4 -> 0; matrix products, arithmetic and copies ran while one was open for 0% -> 0% of each run, Pallas kernels for 0% -> 0%
where the time goes in v3:
time: 85.5 us; the launch traced here: 85.3 us
  Pallas kernels  81.8 us (96%)
  local copies, waits for them, and re-layouts  2.89 us (3%)
    pallas_call x1, Pallas kernels, local(): pl.pallas_call(functools.partial(kernel, nA, nB, nC, nH), out_shape=(jax....  81.8 us
    unnamed x2, local copies, waits for them, and re-layouts  2.89 us

profile of v3, /device:TPU:0, one launch (start us, length us, event | category | flops | bytes accessed | tf_op | source)
XLA Modules:
  0.0 85.3 jit_solution(17061429808042153772)
XLA Ops:
  0.6 81.8 %shard_map.59 = (f32[96]{0:T(128)}, f32[96,1024]{1,0:T(8,128)}) custom-call(bf16[96,1024]{1,0:T(8,128)(2,1)} %hidden.1, bf16[8,1024,512]{2,1,0:T(8,128)(2,1)} %bitcast.1, s32[384]{0:T(512)} %targets.1, f32[384]{0:T(512)} %token_weight.1), custom_call_target="tpu_custom_call" | custom-call | tf_op jit(solution)/shard_map/pallas_call | solution.py:385
  82.5 1.1 %copy.8 = f32[96]{0:T(128)} copy(f32[96]{0:T(128)} %get-tuple-element.4) | data formatting | bytes 768
  83.6 1.8 %copy.9 = f32[96,1024]{1,0:T(8,128)} copy(f32[96,1024]{1,0:T(8,128)} %get-tuple-element.5) | data formatting | bytes 786432

commit v4 on v3

--- a/solution.py
+++ b/solution.py
@@ -311,8 +311,8 @@
         during(i, offset, steps, stage1, 1)
         during(i, offset, steps, stage2, 2)
         during(i, offset, steps, stage3, 3)
-        during(i, 0, steps, finish, 2)
         during(i, 0, steps, multiply, 2)
+        during(i, 0, steps, finish, 1)
         for h in range(nH):
             once(i, (h + 1) * nC + 1, stats_local, h)
             once(i, (h + 1) * nC + 2, stats_plane, h)

time: 85.5 us -> 81.4 us (0.952)
  Pallas kernels: 81.8 us -> 77.7 us
    pallas_call x1, Pallas kernels: 81.8 us -> 77.7 us  [local(): pl.pallas_call(functools.partial(kernel, nA, nB, nC, nH), out_shape=(jax....]
where the time goes in v4:
time: 81.4 us; the launch traced here: 81.2 us
  Pallas kernels  77.7 us (95%)
  local copies, waits for them, and re-layouts  2.89 us (4%)
    pallas_call x1, Pallas kernels, local(): pl.pallas_call(functools.partial(kernel, nA, nB, nC, nH), out_shape=(jax....  77.7 us
    unnamed x2, local copies, waits for them, and re-layouts  2.89 us

profile of v4, /device:TPU:0, one launch (start us, length us, event | category | flops | bytes accessed | tf_op | source)
XLA Modules:
  0.0 81.2 jit_solution(13391226439094333762)
XLA Ops:
  0.6 77.7 %shard_map.59 = (f32[96]{0:T(128)}, f32[96,1024]{1,0:T(8,128)}) custom-call(bf16[96,1024]{1,0:T(8,128)(2,1)} %hidden.1, bf16[8,1024,512]{2,1,0:T(8,128)(2,1)} %bitcast.1, s32[384]{0:T(512)} %targets.1, f32[384]{0:T(512)} %token_weight.1), custom_call_target="tpu_custom_call" | custom-call | tf_op jit(solution)/shard_map/pallas_call | solution.py:385
  78.3 1.1 %copy.8 = f32[96]{0:T(128)} copy(f32[96]{0:T(128)} %get-tuple-element.4) | data formatting | bytes 768
  79.4 1.8 %copy.9 = f32[96,1024]{1,0:T(8,128)} copy(f32[96,1024]{1,0:T(8,128)} %get-tuple-element.5) | data formatting | bytes 786432
